TPU v7x, 32 devices: a whole 2x2x4 slice. The times are simulated.
32 devices in a mesh: dp: 8 (over y, x, core), tp: 4 (over z).
Axes of the slice: x: 2, y: 2, z: 4, core: 2. Of those that a mesh axis runs over, the one named last changes fastest.
Arguments:
- inputs: bfloat16 [26624, 768], P(('dp', 'tp')), may hold values from -6 to 6
- segment_ids: int32 [32, 832], P('dp'), may hold values from -1 to 4, as said below
- mask_flags: int32 [32, 832], P(('dp', 'tp')), may hold values 0 or 1
- mask_token: bfloat16 [768], replicated, may hold values from -6 to 6
- norm_gain: bfloat16 [768], replicated, may hold values from 0.5 to 1.5
- norm_shift: bfloat16 [768], replicated, may hold values from -3 to 3
- heads_weight: bfloat16 [768, 12, 192], P(None, 'tp'), may hold values from -0.21875 to 0.21875
- heads_bias: bfloat16 [12, 128], P('tp'), may hold values from -1.1953125 to 1.1953125
- proj_weight: bfloat16 [768, 768], P('tp'), may hold values from -1.75 to 1.75
- proj_bias: bfloat16 [768], replicated, may hold values from -2 to 2
- attn_scale: bfloat16 [768], replicated, may hold values from 0.5 to 1.5
- mlp_gain: bfloat16 [768], replicated, may hold values from 0.5 to 1.5
- mlp_shift: bfloat16 [768], replicated, may hold values from -3 to 3
- up_weight: bfloat16 [768, 3072], P(None, 'tp'), may hold values from -0.21875 to 0.21875
- up_bias: bfloat16 [3072], P('tp'), may hold values from -2 to 2
- down_weight: bfloat16 [3072, 768], P('tp'), may hold values from -0.109375 to 0.109375
- down_bias: bfloat16 [768], replicated, may hold values from -2 to 2
- mlp_scale: bfloat16 [768], replicated, may hold values from 0.5 to 1.5
- grad_out: bfloat16 [26624, 768], P(('dp', 'tp')), may hold values from -6 to 6
Outputs:
- output: bfloat16 [26624, 768], P(('dp', 'tp'))
- grad_inputs: float32 [26624, 768], P(('dp', 'tp'))
- grad_token: float32 [768], replicated
- grad_norm_gain: float32 [768], replicated
- grad_norm_shift: float32 [768], replicated
- grad_heads_weight: float32 [768, 12, 192], P(None, 'tp')
- grad_heads_bias: float32 [12, 128], P('tp')
- grad_proj_weight: float32 [768, 768], P('tp')
- grad_proj_bias: float32 [768], replicated
- grad_attn_scale: float32 [768], replicated
- grad_mlp_gain: float32 [768], replicated
- grad_mlp_shift: float32 [768], replicated
- grad_up_weight: float32 [768, 3072], P(None, 'tp')
- grad_up_bias: float32 [3072], P('tp')
- grad_down_weight: float32 [3072, 768], P('tp')
- grad_down_bias: float32 [768], replicated
- grad_mlp_scale: float32 [768], replicated
Inputs may be any that keep to these rules, and one draw needn't show every extreme that they name: `segment_ids`: every packed row holds five images numbered 0 to 4 in order from its first slot, then 1 to 32 padding slots marked -1 at its end; each of the first four images has h * w + 1 slots with h and w from 11 to 14, the fifth fills the rest.
All inputs are finite; a program needn't handle non-finite values. No bound on the sum of `mask_flags` on one device may be relied on, other than what follows from the above.
Results may differ from a plain program's by a relative error of at most 0.02.
Values may be sent and summed in bfloat16 or wider, within the bound.
A program may use at most 192 MiB of HBM per device.

v0:
```python
import functools
import jax
import jax.numpy as jnp
from jax import lax
from jax.sharding import PartitionSpec as P

EPSILON = 1e-06
FLOOR_SCORE = -1e30
SQRT_HALF = 0.7071067811865476
INV_ROOT_TWO_PI = 0.3989422804014327


def layer_norm(values, gain, shift):
    centre = values - jnp.mean(values, axis=-1, keepdims=True)
    inverse = lax.rsqrt(jnp.mean(centre * centre, axis=-1, keepdims=True) + EPSILON)
    scaled = centre * inverse
    return (scaled * gain + shift, scaled, inverse)


def norm_back(grad_normed, scaled, inverse, gain):
    grad_scaled = grad_normed * gain
    first = jnp.mean(grad_scaled, axis=-1, keepdims=True)
    second = jnp.mean(grad_scaled * scaled, axis=-1, keepdims=True)
    return inverse * (grad_scaled - first - scaled * second)


def gelu_parts(inner):
    normal_cdf = 0.5 * (1.0 + lax.erf(inner * SQRT_HALF))
    density = jnp.exp(-0.5 * inner * inner) * INV_ROOT_TWO_PI
    return (inner * normal_cdf, normal_cdf + inner * density)


def head_bias_row(bias, head_size):
    blank = jnp.zeros((bias.shape[0], head_size), jnp.float32)
    joined = jnp.concatenate(
        [bias[:, :head_size].astype(jnp.float32), blank, bias[:, head_size:].astype(jnp.float32)],
        axis=1,
    )
    return joined.reshape(-1)


def gather_weight(block, _):
    count = lax.axis_size("dp")
    rows = block.shape[0] // 8
    own = lax.dynamic_slice_in_dim(block, lax.axis_index("dp") % 8 * rows, rows, 0)
    if count == 8:
        return lax.all_gather(own, ("tp", "dp"), axis=0, tiled=True)
    return lax.all_gather(block, "tp", axis=0, tiled=True)


def scatter_grad(partial):
    part = lax.psum_scatter(partial, ("tp", "dp"), scatter_dimension=0, tiled=True)
    return lax.all_gather(part, "dp", axis=0, tiled=True).astype(jnp.float32)


def local(
    inputs,
    segment_ids,
    mask_flags,
    mask_token,
    norm_gain,
    norm_shift,
    heads_weight,
    heads_bias,
    proj_weight,
    proj_bias,
    attn_scale,
    mlp_gain,
    mlp_shift,
    up_weight,
    up_bias,
    down_weight,
    down_bias,
    mlp_scale,
    grad_out,
):
    own_rows, slots = mask_flags.shape
    width = inputs.shape[1]
    triple = heads_weight.shape[2]
    head_size = triple // 3
    scale = head_size ** (-0.5)
    own_ids = lax.dynamic_slice_in_dim(segment_ids, lax.axis_index("tp") * own_rows, own_rows, 0)
    valid = (own_ids.reshape(-1, 1) >= 0).astype(jnp.float32)
    flagged = (mask_flags.reshape(-1, 1) == 1).astype(jnp.float32)
    f32, bf16 = (jnp.float32, jnp.bfloat16)
    dot = functools.partial(lax.dot_general, preferred_element_type=f32)
    nn = (((1,), (0,)), ((), ()))
    nt = (((1,), (1,)), ((), ()))
    tn = (((0,), (0,)), ((), ()))
    heads_all = gather_weight(heads_weight.reshape(width, -1), width // 8)
    proj_all = gather_weight(proj_weight, 0)
    up_all = gather_weight(up_weight, 0)
    down_all = gather_weight(down_weight, 0)
    n_tp = lax.axis_size("tp")
    all_heads_bias = lax.all_gather(heads_bias.astype(f32), "tp", axis=0, tiled=True)
    up_bias_all = lax.all_gather(up_bias.astype(f32), "tp", axis=0, tiled=True)
    heads_now = all_heads_bias.shape[0]
    start_x = valid * (flagged * mask_token.astype(f32) + (1.0 - flagged) * inputs.astype(f32))
    first_gain = norm_gain.astype(f32)
    second_gain = mlp_gain.astype(f32)
    normed1, scaled1, inverse1 = layer_norm(start_x, first_gain, norm_shift.astype(f32))
    normed1 = normed1.astype(bf16)
    heads_cat = jnp.moveaxis(heads_all.reshape(n_tp, width, -1), 0, 1).reshape(width, -1)
    packed = (dot(normed1, heads_cat, nn) + head_bias_row(all_heads_bias, head_size)).astype(bf16)
    blocks = packed.reshape(slots, heads_now, triple)
    query = blocks[..., :head_size]
    keys = blocks[..., head_size : 2 * head_size]
    values = blocks[..., 2 * head_size :]
    groups = own_ids[0]
    same = (groups[:, None] == groups[None, :])[None]
    scores = jnp.einsum("qhd,khd->hqk", query, keys, preferred_element_type=f32) * scale
    scores = jnp.where(same, scores, FLOOR_SCORE)
    largest = jnp.max(scores, axis=-1, keepdims=True)
    raised = jnp.exp(scores - largest)
    total = jnp.sum(raised, axis=-1, keepdims=True)
    shares = (raised / total).astype(bf16)
    mixed = jnp.einsum("hqk,khd->qhd", shares, values, preferred_element_type=f32).astype(bf16)
    mixed = mixed.reshape(slots, -1)
    branch1 = dot(mixed, proj_all, nn) + proj_bias.astype(f32)
    middle = start_x + attn_scale.astype(f32) * branch1
    normed2, scaled2, inverse2 = layer_norm(middle, second_gain, mlp_shift.astype(f32))
    normed2 = normed2.astype(bf16)
    up_cat = jnp.moveaxis(up_all.reshape(n_tp, width, -1), 0, 1).reshape(width, -1)
    unit_input = dot(normed2, up_cat, nn) + up_bias_all
    unit_value, derivative = gelu_parts(unit_input)
    unit_low = unit_value.astype(bf16)
    branch2 = dot(unit_low, down_all, nn) + down_bias.astype(f32)
    output = (valid * (middle + mlp_scale.astype(f32) * branch2)).astype(bf16)
    grad_final = valid * grad_out.astype(f32)
    grad_scale2 = jnp.sum(branch2 * grad_final, axis=0)
    grad_branch2 = mlp_scale.astype(f32) * grad_final
    grad_down_bias = jnp.sum(grad_branch2, axis=0)
    grad_low2 = grad_branch2.astype(bf16)
    sum_down = scatter_grad(dot(unit_low, grad_low2, tn).astype(bf16))
    grad_unit = (dot(grad_low2, down_all, nt) * derivative).astype(bf16)
    columns = lambda g: jnp.moveaxis(g.reshape(width, n_tp, -1), 1, 0).reshape(n_tp * width, -1)
    sum_up = scatter_grad(columns(dot(normed2, grad_unit, tn).astype(bf16)))
    grad_up_bias = jnp.sum(grad_unit, axis=0, dtype=f32)
    grad_normed2 = dot(grad_unit, up_cat, nt)
    grad_gain2 = jnp.sum(grad_normed2 * scaled2, axis=0)
    grad_shift2 = jnp.sum(grad_normed2, axis=0)
    grad_middle = grad_final + norm_back(grad_normed2, scaled2, inverse2, second_gain)
    grad_scale1 = jnp.sum(branch1 * grad_middle, axis=0)
    grad_branch1 = attn_scale.astype(f32) * grad_middle
    grad_proj_bias = jnp.sum(grad_branch1, axis=0)
    grad_low1 = grad_branch1.astype(bf16)
    sum_proj = scatter_grad(dot(mixed, grad_low1, tn).astype(bf16))
    grad_mixed = dot(grad_low1, proj_all, nt).astype(bf16).reshape(slots, heads_now, head_size)
    exact = raised / total
    grad_shares = jnp.einsum("qhd,khd->hqk", grad_mixed, values, preferred_element_type=f32)
    centre = jnp.sum(exact * grad_shares, axis=-1, keepdims=True)
    grad_scores = (exact * (grad_shares - centre)).astype(bf16)
    grad_query = jnp.einsum("hqk,khd->qhd", grad_scores, keys, preferred_element_type=f32) * scale
    grad_keys = jnp.einsum("hqk,qhd->khd", grad_scores, query, preferred_element_type=f32) * scale
    grad_values = jnp.einsum("hqk,qhd->khd", shares, grad_mixed, preferred_element_type=f32)
    grad_packed = jnp.concatenate([grad_query, grad_keys, grad_values], axis=-1).astype(bf16)
    grad_packed = grad_packed.reshape(slots, -1)
    sum_heads = scatter_grad(columns(dot(normed1, grad_packed, tn).astype(bf16)))
    sum_heads = sum_heads.reshape(heads_weight.shape)
    bias_sums = jnp.sum(grad_packed, axis=0, dtype=f32).reshape(heads_now, triple)
    grad_normed1 = dot(grad_packed, heads_cat, nt)
    grad_gain1 = jnp.sum(grad_normed1 * scaled1, axis=0)
    grad_shift1 = jnp.sum(grad_normed1, axis=0)
    grad_start = grad_middle + norm_back(grad_normed1, scaled1, inverse1, first_gain)
    grad_inputs = valid * (1.0 - flagged) * grad_start
    grad_token = jnp.sum(valid * flagged * grad_start, axis=0)
    small = jnp.concatenate(
        [
            grad_token,
            grad_gain1,
            grad_shift1,
            grad_proj_bias,
            grad_scale1,
            grad_gain2,
            grad_shift2,
            grad_down_bias,
            grad_scale2,
            bias_sums.reshape(-1),
            grad_up_bias,
        ]
    )
    small = lax.psum(small, ("dp", "tp"))
    (
        sum_token,
        sum_gain1,
        sum_shift1,
        sum_proj_bias,
        sum_scale1,
        sum_gain2,
        sum_shift2,
        sum_down_bias,
        sum_scale2,
    ) = [small[i * width : (i + 1) * width] for i in range(9)]
    me = lax.axis_index("tp")
    bias_sums = small[9 * width : 9 * width + heads_now * triple].reshape(heads_now, triple)
    bias_sums = lax.dynamic_slice_in_dim(
        bias_sums, me * heads_bias.shape[0], heads_bias.shape[0], 0
    )
    sum_heads_bias = jnp.concatenate(
        [bias_sums[:, :head_size], bias_sums[:, 2 * head_size :]], axis=1
    )
    sum_up_bias = lax.dynamic_slice_in_dim(
        small[9 * width + heads_now * triple :], me * up_bias.shape[0], up_bias.shape[0], 0
    )
    return (
        output,
        grad_inputs,
        sum_token,
        sum_gain1,
        sum_shift1,
        sum_heads,
        sum_heads_bias,
        sum_proj,
        sum_proj_bias,
        sum_scale1,
        sum_gain2,
        sum_shift2,
        sum_up,
        sum_up_bias,
        sum_down,
        sum_down_bias,
        sum_scale2,
    )


def solution(mesh):
    placed = (
        P(("dp", "tp"), None),
        P("dp", None),
        P(("dp", "tp"), None),
        P(),
        P(),
        P(),
        P(None, "tp", None),
        P("tp", None),
        P("tp", None),
        P(),
        P(),
        P(),
        P(),
        P(None, "tp"),
        P("tp"),
        P("tp", None),
        P(),
        P(),
        P(("dp", "tp"), None),
    )
    return jax.shard_map(
        local,
        mesh=mesh,
        in_specs=placed,
        out_specs=(
            P(("dp", "tp"), None),
            P(("dp", "tp"), None),
            P(),
            P(),
            P(),
            P(None, "tp", None),
            P("tp", None),
            P("tp", None),
            P(),
            P(),
            P(),
            P(),
            P(None, "tp"),
            P("tp"),
            P("tp", None),
            P(),
            P(),
        ),
        check_vma=False,
    )
```

profile of v0, /device:TPU:0, one launch (start us, length us, event | category | flops | bytes accessed | tf_op | source)
XLA Modules:
  0.0 799.6 jit_solution(7235926682024903587)
XLA Ops:
  7.4 1.2 constant_dynamic-slice_fusion.3
  8.6 0.8 copy.81
  9.5 1.4 constant_dynamic-slice_fusion.2
  10.9 0.7 constant_dynamic-slice_fusion.1
  11.7 1.6 constant_dynamic-slice_fusion
  13.4 0.7 compare_reduce_fusion
  14.1 0.7 dynamic-slice_reduce_fusion
  16.8 13.5 %all-gather = f32[4,3,128]{2,1,0:T(4,128)S(1)} all-gather(f32[1,3,128]{2,1,0:T(4,128)S(1)} %bitcast_convert_fusion), channel_id=1, replica_groups=mesh['dp'=8,'tp'=4] {'tp'}, dimensions={0}, use_global_device_ids=true | all-gather | bytes 7680 | tf_op jit(solution)/shard_map/all_gather | solution.py:95
  30.3 0.8 fusion.21
  31.2 0.9 multiply_reduce_fusion.9
  32.4 13.2 %all-gather.1 = f32[4,1,768]{2,1,0:T(1,128)S(1)} all-gather(f32[1,1,768]{2,1,0:T(1,128)S(1)} %reshape.247), channel_id=1, replica_groups=mesh['dp'=8,'tp'=4] {'tp'}, dimensions={0}, use_global_device_ids=true | all-gather | bytes 15360 | tf_op jit(solution)/shard_map/all_gather | solution.py:96
  45.6 30.0 %all-gather.9.cloned.1.call-done = bf16[3072,576]{1,0:T(8,128)(2,1)} async-done(((bf16[96,576]{1,0:T(8,128)(2,1)}), bf16[3072,576]{1,0:T(8,128)(2,1)}) %all-gather.9.cloned.1.call-update) | async-done | bytes 3538960 | tf_op jit(solution)/shard_map/all_gather | solution.py:47
  75.6 8.0 %copy.100 = bf16[4,768,576]{1,0,2:T(4,128)(2,1)} copy(bf16[4,768,576]{2,1,0:T(8,128)(2,1)} %bitcast.70) | data formatting | bytes 7077888 | tf_op jit(solution)/shard_map/reshape | solution.py:103
  83.6 2.5 copy.83
  86.1 1.7 copy-done.11
  87.8 5.3 add_convert_fusion
  93.1 6.3 copy.84
  99.5 19.8 %fusion.53 = (f32[12,832]{1,0:T(8,128)S(1)}, f32[12,832,832]{1,2,0:T(8,128)}) fusion(pred[832,832]{0,1:T(8,128)(4,1)S(1)} %broadcast_compare_fusion, bf16[832,12,192]{0,2,1:T(8,128)(2,1)} %bitcast.56), kind=kOutput, calls=%fused_computation.116 | convolution fusion | flops 1096483584 | bytes 36711424 | tf_op jit(solution)/shard_map/sub | solution.py:114
  119.2 16.0 %fusion.26 = bf16[12,64,832]{2,1,0:T(8,128)(2,1)} fusion(bf16[832,12,192]{0,2,1:T(8,128)(2,1)} %bitcast.57, f32[12,832,832]{1,2,0:T(8,128)} %get-tuple-element.74, f32[12,832]{1,0:T(8,128)S(1)} %get-tuple-element.73), kind=kOutput, calls=%fused_computation.62 | convolution fusion | flops 1080508416 | bytes 38476800 | tf_op jit(solution)/shard_map/hqk,khd->qhd/dot_general | solution.py:117
  135.3 4.9 fusion.50
  140.2 1.4 copy-done.4
  142.1 55.8 %all-gather.13.cloned.1.call-done = bf16[3072,768]{1,0:T(8,128)(2,1)} async-done(((bf16[96,768]{1,0:T(8,128)(2,1)}), bf16[3072,768]{1,0:T(8,128)(2,1)}) %all-gather.13.cloned.1.call-update) | async-done | bytes 4718608 | tf_op jit(solution)/shard_map/all_gather | solution.py:47
  197.9 6.6 copy.86
  204.5 10.7 %multiply_convert_fusion.1 = (bf16[832,3072]{1,0:T(8,128)(2,1)}, f32[832,3072]{1,0:T(8,128)}) fusion(f32[3072]{0:T(1024)S(1)} %bitcast.77, bf16[768,3072]{0,1:T(8,128)(2,1)} %bitcast.64, f32[832,768]{1,0:T(8,128)} %copy-done.4, f32[768]{0:T(1024)S(1)} %convert_element_type.165, f32[768]{0:T(1024)S(1)} %convert_element_type.164, f32[832]{0:T(1024)S(1)} %add_rsqrt_fusion, ...), kind=kOutput, calls=%fused_computation.18 | convolution fusion | flops 3944398848 | bytes 22635008 | tf_op jit(solution)/shard_map/dot_general | solution.py:124
  215.2 48.5 %all-gather.15.cloned.1.call-done = bf16[3072,768]{1,0:T(8,128)(2,1)} async-done(((bf16[96,768]{1,0:T(8,128)(2,1)}), bf16[3072,768]{1,0:T(8,128)(2,1)}) %all-gather.15.cloned.1.call-update) | async-done | bytes 4718608 | tf_op jit(solution)/shard_map/all_gather | solution.py:47
  263.7 11.2 %convert_reduce_fusion = (f32[3072]{0:T(1024)}, bf16[832,3072]{1,0:T(8,128)(2,1)S(1)}) fusion(f32[832,3072]{1,0:T(8,128)} %get-tuple-element.80, f32[3072]{0:T(1024)S(1)} %bitcast.78, bf16[3072,768]{1,0:T(8,128)(2,1)} %all-gather.15.cloned.1.call-done, bf16[832,768]{1,0:T(8,128)(2,1)S(1)} %copy-done.13, f32[768]{0:T(1024)S(1)} %convert_element_type.163, ...), kind=kOutput, calls=%fused_computation.17 | convolution fusion | flops 3961648128 | bytes 21362944 | tf_op jit(solution)/shard_map/dot_general | solution.py:135
  274.9 6.6 multiply_reduce_fusion.2
  281.5 7.7 convolution_convert_fusion.1
  289.1 7.1 convolution_convert_fusion
  296.2 9.7 %reshape.241 = bf16[768,4,768]{2,1,0:T(4,128)(2,1)} reshape(bf16[768,3072]{1,0:T(8,128)(2,1)} %convolution_convert_fusion.1) | data formatting | bytes 9437184 | tf_op jit(solution)/shard_map/reshape | solution.py:136
  306.0 5.1 copy.95
  311.2 4.9 multiply_reduce_fusion.3
  316.1 1.4 copy-done.6
  317.5 2.3 convolution_convert_fusion.3
  319.8 1.8 copy.87
  321.6 27.2 %multiply_reduce_fusion = (f32[12,832]{1,0:T(8,128)S(1)}, f32[12,832,832]{1,2,0:T(8,128)}) fusion(f32[12,832,832]{1,2,0:T(8,128)} %get-tuple-element.74, f32[12,832]{1,0:T(8,128)S(1)} %get-tuple-element.73, bf16[832,12,64]{0,2,1:T(8,128)(2,1)S(1)} %bitcast.74, bf16[832,12,192]{0,2,1:T(8,128)(2,1)} %bitcast.58), kind=kOutput, calls=%fused_computation.2 | convolution fusion | flops 1088166144 | bytes 71743488 | tf_op jit(solution)/shard_map/qhd,khd->hqk/dot_general | solution.py:150
  348.9 30.1 %multiply_convert_fusion = bf16[12,832,832]{1,2,0:T(8,128)(2,1)} fusion(f32[12,832,832]{1,2,0:T(8,128)} %get-tuple-element.78, f32[12,832]{1,0:T(8,128)S(1)} %get-tuple-element.77, f32[12,832,832]{1,2,0:T(8,128)} %get-tuple-element.74, f32[12,832]{1,0:T(8,128)S(1)} %get-tuple-element.73), kind=kLoop, calls=%fused_computation.1 | loop fusion | flops 33226752 | bytes 83146752 | tf_op jit(solution)/shard_map/convert_element_type | solution.py:152
  378.9 3.8 convolution_convert_fusion.4
  382.7 10.4 %multiply_bitcast_fusion = bf16[832,12,64]{0,2,1:T(8,128)(2,1)} fusion(bf16[12,832,832]{1,2,0:T(8,128)(2,1)} %multiply_convert_fusion, bf16[832,12,192]{0,2,1:T(8,128)(2,1)} %bitcast.59), kind=kOutput, calls=%fused_computation.31 | convolution fusion | flops 1064534016 | bytes 20545536 | tf_op jit(solution)/shard_map/hqk,qhd->khd/dot_general | solution.py:154
  393.1 15.3 %fusion.23 = bf16[832,12,64]{0,2,1:T(8,128)(2,1)} fusion(bf16[832,12,64]{0,2,1:T(8,128)(2,1)S(1)} %bitcast.75, f32[12,832,832]{1,2,0:T(8,128)} %get-tuple-element.74, f32[12,832]{1,0:T(8,128)S(1)} %get-tuple-element.73), kind=kOutput, calls=%fused_computation.61 | convolution fusion | flops 1079869440 | bytes 35822592 | tf_op jit(solution)/shard_map/hqk,qhd->khd/dot_general | solution.py:155
  408.5 10.0 %multiply_bitcast_fusion.1 = bf16[832,12,64]{0,2,1:T(8,128)(2,1)S(1)} fusion(bf16[12,832,832]{1,2,0:T(8,128)(2,1)} %multiply_convert_fusion, bf16[832,12,192]{0,2,1:T(8,128)(2,1)} %bitcast.60), kind=kOutput, calls=%fused_computation.32 | convolution fusion | flops 1064534016 | bytes 20545536 | tf_op jit(solution)/shard_map/hqk,khd->qhd/dot_general | solution.py:153
  418.6 1.1 convert_reduce_fusion.1
  419.7 1.9 copy-done.10
  421.7 6.5 convolution_convert_fusion.2
  428.2 5.8 copy.91
  434.0 6.0 copy.103
  440.8 9.7 %fusion.62 = f32[832,768]{1,0:T(8,128)} fusion(bf16[832,3072]{1,0:T(8,128)(2,1)} %get-tuple-element.79, bf16[3072,768]{1,0:T(8,128)(2,1)} %all-gather.15.cloned.1.call-done), kind=kOutput, calls=%fused_computation.117 | convolution fusion | flops 3925868544 | bytes 12386304 | tf_op jit(solution)/shard_map/dot_general | solution.py:127
  450.8 11.5 %multiply_reduce_fusion.4 = (f32[768]{0:T(1024)S(1)}, f32[832]{0:T(1024)S(1)}, f32[832]{0:T(1024)S(1)}, f32[768]{0:T(1024)S(1)}, f32[768]{0:T(1024)S(1)}, /*inde...) fusion(bf16[832,768]{1,0:T(8,128)(2,1)S(1)} %copy-done.3, f32[832]{0:T(1024)S(1)} %copy-done.30, ...), kind=kOutput, calls=%fused_computation.36 | convolution fusion | flops 2960371200 | bytes 18922240 | tf_op jit(solution)/shard_map/dot_general | solution.py:161
  462.4 2.9 multiply_reduce_fusion.5
  465.3 64.1 %reduce-scatter.11.cloned.1.call-done = bf16[96,768]{1,0:T(8,128)(2,1)} async-done(((bf16[3072,768]{1,0:T(8,128)(2,1)}), bf16[96,768]{1,0:T(8,128)(2,1)}) %reduce-scatter.11.cloned.1.call-update) | async-done | bytes 147472 | tf_op jit(solution)/shard_map/reduce_scatter | solution.py:52
  529.6 40.5 %psum.7 = f32[12288]{0:T(1024)S(1)} all-reduce(f32[12288]{0:T(1024)S(1)} %constant_dynamic-update-slice_fusion), channel_id=1, replica_groups=mesh['dp'=8,'tp'=4] {'dp','tp'}, use_global_device_ids=true, to_apply=%region_22.23 | all-reduce | flops 12288 | bytes 98304 | tf_op jit(solution)/shard_map/psum | solution.py:182
  570.2 0.7 dynamic_slice.27
  570.9 0.7 pad_maximum_fusion.1
  572.2 3.4 broadcast_multiply_fusion
  575.6 54.7 %reduce-scatter.7.cloned.1.call-done = bf16[24,768]{1,0:T(8,128)(2,1)} async-done(((bf16[768,768]{1,0:T(8,128)(2,1)}), bf16[24,768]{1,0:T(8,128)(2,1)}) %reduce-scatter.7.cloned.1.call-update) | async-done | bytes 36880 | tf_op jit(solution)/shard_map/reduce_scatter | solution.py:52
  630.4 9.5 %all_gather.37 = bf16[192,768]{1,0:T(8,128)(2,1)S(1)} all-gather(bf16[24,768]{1,0:T(8,128)(2,1)} %reduce-scatter.7.cloned.1.call-done), channel_id=1, replica_groups=mesh['dp'=8,'tp'=4] {'dp'}, dimensions={0}, use_global_device_ids=true | all-gather | bytes 331776 | tf_op jit(solution)/shard_map/all_gather | solution.py:53
  639.9 0.9 convert_element_type.183
  640.8 98.1 %reduce-scatter.13.cloned.1.call-done = bf16[96,576]{1,0:T(8,128)(2,1)} async-done(((bf16[3072,576]{1,0:T(8,128)(2,1)}), bf16[96,576]{1,0:T(8,128)(2,1)}) %reduce-scatter.13.cloned.1.call-update) | async-done | bytes 110608 | tf_op jit(solution)/shard_map/reduce_scatter | solution.py:52
  738.8 10.8 %all_gather.36 = bf16[768,576]{1,0:T(8,128)(2,1)S(1)} all-gather(bf16[96,576]{1,0:T(8,128)(2,1)} %reduce-scatter.13.cloned.1.call-done), channel_id=1, replica_groups=mesh['dp'=8,'tp'=4] {'dp'}, dimensions={0}, use_global_device_ids=true | all-gather | bytes 995328 | tf_op jit(solution)/shard_map/all_gather | solution.py:53
  750.3 1.4 convert.2
  751.7 12.1 %all-gather.17.cloned.1.call-done = bf16[768,768]{1,0:T(8,128)(2,1)} async-done(((bf16[96,768]{1,0:T(8,128)(2,1)}), bf16[768,768]{1,0:T(8,128)(2,1)}) %all-gather.17.cloned.1.call-update) | async-done | bytes 1179664 | tf_op jit(solution)/shard_map/all_gather | solution.py:53
  763.8 2.9 convert_element_type.185
  766.7 22.9 %all-gather.19.cloned.1.call-done = bf16[768,768]{1,0:T(8,128)(2,1)} async-done(((bf16[96,768]{1,0:T(8,128)(2,1)}), bf16[768,768]{1,0:T(8,128)(2,1)}) %all-gather.19.cloned.1.call-update) | async-done | bytes 1179664 | tf_op jit(solution)/shard_map/all_gather | solution.py:53
  789.6 2.8 convert_element_type.187
  (176 shorter events, 5.7 us)
Async XLA Ops:
  7.2 3.7 copy-start
  7.2 9.3 %copy-start.49 = (bf16[3,128]{1,0:T(4,128)(2,1)S(1)}, bf16[3,128]{1,0:T(4,128)(2,1)}, u32[]{:S(2)}) copy-start(bf16[3,128]{1,0:T(4,128)(2,1)} %param.26) | copy-start | bytes 2308
  7.2 9.3 %copy-start.48 = (bf16[768]{0:T(1024)(128)(2,1)S(1)}, bf16[768]{0:T(1024)(128)(2,1)}, u32[]{:S(2)}) copy-start(bf16[768]{0:T(1024)(128)(2,1)} %param.33) | copy-start | bytes 4612
  7.2 9.3 %copy-start.39 = (bf16[768]{0:T(1024)(128)(2,1)S(1)}, bf16[768]{0:T(1024)(128)(2,1)}, u32[]{:S(2)}) copy-start(bf16[768]{0:T(1024)(128)(2,1)} %param.22) | copy-start | bytes 4612
  7.2 9.3 %copy-start.40 = (bf16[768]{0:T(1024)(128)(2,1)S(1)}, bf16[768]{0:T(1024)(128)(2,1)}, u32[]{:S(2)}) copy-start(bf16[768]{0:T(1024)(128)(2,1)} %param.23) | copy-start | bytes 4612
  7.3 9.4 %copy-start.41 = (bf16[768]{0:T(1024)(128)(2,1)S(1)}, bf16[768]{0:T(1024)(128)(2,1)}, u32[]{:S(2)}) copy-start(bf16[768]{0:T(1024)(128)(2,1)} %param.29) | copy-start | bytes 4612
  7.3 9.4 %copy-start.42 = (bf16[768]{0:T(1024)(128)(2,1)S(1)}, bf16[768]{0:T(1024)(128)(2,1)}, u32[]{:S(2)}) copy-start(bf16[768]{0:T(1024)(128)(2,1)} %param.30) | copy-start | bytes 4612
  7.3 9.4 %copy-start.43 = (bf16[768]{0:T(1024)(128)(2,1)S(1)}, bf16[768]{0:T(1024)(128)(2,1)}, u32[]{:S(2)}) copy-start(bf16[768]{0:T(1024)(128)(2,1)} %param.36) | copy-start | bytes 4612
  7.3 9.4 %copy-start.44 = (bf16[768]{0:T(1024)(128)(2,1)S(1)}, bf16[768]{0:T(1024)(128)(2,1)}, u32[]{:S(2)}) copy-start(bf16[768]{0:T(1024)(128)(2,1)} %param.24) | copy-start | bytes 4612
  7.3 9.4 %copy-start.45 = (bf16[768]{0:T(1024)(128)(2,1)S(1)}, bf16[768]{0:T(1024)(128)(2,1)}, u32[]{:S(2)}) copy-start(bf16[768]{0:T(1024)(128)(2,1)} %param.28) | copy-start | bytes 4612
  7.3 9.5 %copy-start.46 = (bf16[768]{0:T(1024)(128)(2,1)S(1)}, bf16[768]{0:T(1024)(128)(2,1)}, u32[]{:S(2)}) copy-start(bf16[768]{0:T(1024)(128)(2,1)} %param.31) | copy-start | bytes 4612
  7.3 23.0 %copy-start.2 = (bf16[832,768]{1,0:T(8,128)(2,1)S(1)}, bf16[832,768]{1,0:T(8,128)(2,1)}, u32[]{:S(2)}) copy-start(bf16[832,768]{1,0:T(8,128)(2,1)} %param.19) | copy-start | bytes 3833860
  7.3 68.2 %all-gather.9.cloned.1.call-start = ((), (), s32[]{:S(2)}) async-start(), calls=%async_computation.4 | async-start | bytes 4055040 | tf_op jit(solution)/shard_map/all_gather | solution.py:47
  9.4 125.8 %all-gather.11.cloned.1.call-start = ((), (), s32[]{:S(2)}) async-start(), calls=%async_computation.5 | async-start | bytes 1216512 | tf_op jit(solution)/shard_map/all_gather | solution.py:47
  10.9 187.0 %all-gather.13.cloned.1.call-start = ((), (), s32[]{:S(2)}) async-start(), calls=%async_computation.6 | async-start | bytes 4866048 | tf_op jit(solution)/shard_map/all_gather | solution.py:47
  11.7 252.0 %all-gather.15.cloned.1.call-start = ((), (), s32[]{:S(2)}) async-start(), calls=%async_computation.7 | async-start | bytes 4866048 | tf_op jit(solution)/shard_map/all_gather | solution.py:47
  13.3 437.2 %reduce-scatter.9.cloned.1.call-start = ((), (), s32[]{:S(2)}) async-start(), calls=%async_computation.9 | async-start | bytes 4866048 | tf_op jit(solution)/shard_map/reduce_scatter | solution.py:52
  14.1 121.2 %copy-start.16 = (f32[832]{0:T(1024)}, f32[832]{0:T(1024)S(1)}, u32[]{:S(2)}) copy-start(f32[832]{0:T(1024)S(1)} %convert_element_type.150) | copy-start | bytes 9988
  15.4 295.7 %copy-start.14 = (f32[832]{0:T(1024)}, f32[832]{0:T(1024)S(1)}, u32[]{:S(2)}) copy-start(f32[832]{0:T(1024)S(1)} %convert_element_type.149) | copy-start | bytes 9988
  16.0 119.2 %copy-start.18 = (f32[832]{0:T(1024)}, f32[832]{0:T(1024)S(1)}, u32[]{:S(2)}) copy-start(f32[832]{0:T(1024)S(1)} %get-tuple-element.72) | copy-start | bytes 9988
  16.6 118.7 %copy-start.20 = (f32[768]{0:T(1024)}, f32[768]{0:T(1024)S(1)}, u32[]{:S(2)}) copy-start(f32[768]{0:T(1024)S(1)} %convert_element_type.151) | copy-start | bytes 9220
  16.6 69.4 %copy-start.27 = (f32[768]{0:T(1024)}, f32[768]{0:T(1024)S(1)}, u32[]{:S(2)}) copy-start(f32[768]{0:T(1024)S(1)} %convert_element_type.154) | copy-start | bytes 9220
  16.7 272.4 %copy-start.33 = (f32[768]{0:T(1024)}, f32[768]{0:T(1024)S(1)}, u32[]{:S(2)}) copy-start(f32[768]{0:T(1024)S(1)} %convert_element_type.163) | copy-start | bytes 9220
  16.7 69.3 %copy-start.35 = (f32[768]{0:T(1024)}, f32[768]{0:T(1024)S(1)}, u32[]{:S(2)}) copy-start(f32[768]{0:T(1024)S(1)} %convert_element_type.155) | copy-start | bytes 9220
  31.1 54.9 %copy-start.22 = (f32[832]{0:T(1024)}, f32[832]{0:T(1024)S(1)}, u32[]{:S(2)}) copy-start(f32[832]{0:T(1024)S(1)} %broadcast_multiply_fusion.6) | copy-start | bytes 9988
  32.1 54.0 %copy-start.29 = (f32[832]{0:T(1024)}, f32[832]{0:T(1024)S(1)}, u32[]{:S(2)}) copy-start(f32[832]{0:T(1024)S(1)} %add_rsqrt_fusion.1) | copy-start | bytes 9988
  86.1 1.8 copy-start.11
  140.2 1.4 copy-start.4
  204.5 59.2 %copy-start.13 = (bf16[832,768]{1,0:T(8,128)(2,1)S(1)}, bf16[832,768]{1,0:T(8,128)(2,1)}, u32[]{:S(2)}) copy-start(bf16[832,768]{1,0:T(8,128)(2,1)} %param.37) | copy-start | bytes 3833860
  204.5 70.3 %slice-start = ((s8[4718592]{0:T(1024)(128)(4,1)}), s8[524288]{0:T(1024)(128)(4,1)S(1)}, s32[]{:S(2)}) async-start(s8[4718592]{0:T(1024)(128)(4,1)} %bitcast.65), calls=%async_computation.14 | async-start | bytes 1048576
  263.7 11.2 %copy-start.5 = (f32[832,768]{1,0:T(8,128)S(1)}, f32[832,768]{1,0:T(8,128)}, u32[]{:S(2)}) copy-start(f32[832,768]{1,0:T(8,128)} %copy-done.4) | copy-start | bytes 7667716
  263.7 11.2 %slice-start.1 = ((s8[4718592]{0:T(1024)(128)(4,1)}), s8[4194304]{0:T(1024)(128)(4,1)S(1)}, s32[]{:S(2)}) async-start(s8[4718592]{0:T(1024)(128)(4,1)} %bitcast.65), calls=%async_computation.15 | async-start | bytes 8388608
  281.5 7.7 copy-start.51
  311.1 218.3 %reduce-scatter.11.cloned.1.call-start = ((), (), s32[]{:S(2)}) async-start(), calls=%async_computation.11 | async-start | bytes 4866048 | tf_op jit(solution)/shard_map/reduce_scatter | solution.py:52
  311.2 6.4 copy-start.50
  316.1 1.4 copy-start.6
  348.8 281.6 %reduce-scatter.7.cloned.1.call-start = ((), (), s32[]{:S(2)}) async-start(), calls=%async_computation.8 | async-start | bytes 1216512 | tf_op jit(solution)/shard_map/reduce_scatter | solution.py:52
  348.9 30.1 %copy-start.7 = (f32[832,768]{1,0:T(8,128)S(1)}, f32[832,768]{1,0:T(8,128)}, u32[]{:S(2)}) copy-start(f32[832,768]{1,0:T(8,128)} %copy-done.6) | copy-start | bytes 7667716
  408.5 330.4 %reduce-scatter.13.cloned.1.call-start = ((), (), s32[]{:S(2)}) async-start(), calls=%async_computation.13 | async-start | bytes 4055040 | tf_op jit(solution)/shard_map/reduce_scatter | solution.py:52
  408.5 10.0 %copy-start.9 = (bf16[832,12,64]{0,2,1:T(8,128)(2,1)S(1)}, bf16[832,12,64]{0,2,1:T(8,128)(2,1)}, u32[]{:S(2)}) copy-start(bf16[832,12,64]{0,2,1:T(8,128)(2,1)} %multiply_bitcast_fusion) | copy-start | bytes 3833860
  408.5 10.0 %copy-start.12 = (bf16[832,12,64]{0,2,1:T(8,128)(2,1)S(1)}, bf16[832,12,64]{0,2,1:T(8,128)(2,1)}, u32[]{:S(2)}) copy-start(bf16[832,12,64]{0,2,1:T(8,128)(2,1)} %fusion.23) | copy-start | bytes 3833860
  418.5 3.1 copy-start.3
  418.5 3.1 copy-start.15
  418.6 3.1 copy-start.17
  418.6 3.1 copy-start.19
  418.6 3.1 copy-start.21
  418.6 3.1 copy-start.23
  418.6 3.1 copy-start.28
  418.6 3.1 copy-start.30
  418.6 3.1 copy-start.36
  419.7 1.9 copy-start.10
  440.0 0.7 copy-start.47
  440.0 323.8 %all-gather.17.cloned.1.call-start = ((), (), s32[]{:S(2)}) async-start(), calls=%async_computation.10 | async-start | bytes 1327104 | tf_op jit(solution)/shard_map/all_gather | solution.py:53
  440.8 10.0 %copy-start.34 = (f32[768]{0:T(1024)S(1)}, f32[768]{0:T(1024)}, u32[]{:S(2)}) copy-start(f32[768]{0:T(1024)} %copy-done.33) | copy-start | bytes 9220
  450.5 11.8 %copy-start.26 = (f32[832]{0:T(1024)S(1)}, f32[832]{0:T(1024)}, u32[]{:S(2)}) copy-start(f32[832]{0:T(1024)} %get-tuple-element.53) | copy-start | bytes 9988
  450.5 339.1 %all-gather.19.cloned.1.call-start = ((), (), s32[]{:S(2)}) async-start(), calls=%async_computation.12 | async-start | bytes 1327104 | tf_op jit(solution)/shard_map/all_gather | solution.py:53
  450.8 11.5 %copy-start.8 = (f32[832,768]{1,0:T(8,128)S(1)}, f32[832,768]{1,0:T(8,128)}, u32[]{:S(2)}) copy-start(f32[832,768]{1,0:T(8,128)} %copy-done.6) | copy-start | bytes 7667716
  462.3 67.1 %copy-start.25 = (f32[768]{0:T(1024)S(1)}, f32[768]{0:T(1024)}, u32[]{:S(2)}) copy-start(f32[768]{0:T(1024)} %get-tuple-element.42) | copy-start | bytes 9220
  462.3 67.1 %copy-start.24 = (f32[768]{0:T(1024)S(1)}, f32[768]{0:T(1024)}, u32[]{:S(2)}) copy-start(f32[768]{0:T(1024)} %get-tuple-element.41) | copy-start | bytes 9220
  462.3 67.1 %copy-start.38 = (f32[768]{0:T(1024)S(1)}, f32[768]{0:T(1024)}, u32[]{:S(2)}) copy-start(f32[768]{0:T(1024)} %get-tuple-element.34) | copy-start | bytes 9220
  462.3 67.2 %copy-start.37 = (f32[768]{0:T(1024)S(1)}, f32[768]{0:T(1024)}, u32[]{:S(2)}) copy-start(f32[768]{0:T(1024)} %get-tuple-element.40) | copy-start | bytes 9220
  462.4 67.2 %copy-start.32 = (f32[3072]{0:T(1024)S(1)}, f32[3072]{0:T(1024)}, u32[]{:S(2)}) copy-start(f32[3072]{0:T(1024)} %get-tuple-element.82) | copy-start | bytes 36868
  462.4 109.8 %copy-start.31 = (f32[832]{0:T(1024)S(1)}, f32[832]{0:T(1024)}, u32[]{:S(2)}) copy-start(f32[832]{0:T(1024)} %get-tuple-element.71) | copy-start | bytes 9988
  763.8 28.7 %copy-start.1 = (bf16[768,768]{1,0:T(8,128)(2,1)S(1)}, bf16[768,768]{1,0:T(8,128)(2,1)}, u32[]{:S(2)}) copy-start(bf16[768,768]{1,0:T(8,128)(2,1)} %param.32) | copy-start | bytes 3538948
Sparse Core Ops, SparseCore 0:
  11.6 63.8 all-gather.8
  79.0 52.6 all-gather.10
  135.2 62.5 all-gather.12
  201.2 62.4 all-gather.14
  311.2 105.7 reduce-scatter.8
  423.3 106.0 reduce-scatter.10
  535.0 95.2 reduce-scatter.6
  635.8 103.0 reduce-scatter.12
  740.7 23.0 all-gather.16
  765.5 24.0 all-gather.18
where the time goes:
time: 804 us; the launch traced here: 800 us
  waiting for transfers between devices  386 us (48%)
  matrix products  186 us (23%)
  blocking collectives  87.6 us (11%)
  local copies, waits for them, and re-layouts  68.1 us (8%)
  other arithmetic  55.7 us (7%)
  between operations  15.4 us (2%)
    reduce_scatter x4, waiting for transfers between devices, scatter_grad(): lax.psum_scatter(partial, ('tp', 'dp'), scatter_dimension=0, tiled=True)  217 us
    all_gather x4, waiting for transfers between devices, gather_weight(): return lax.all_gather(own, ('tp', 'dp'), axis=0, tiled=True)  134 us
    psum x1, blocking collectives, local(): small = lax.psum(small, ('dp', 'tp'))  40.5 us
    all_gather x2, waiting for transfers between devices, scatter_grad(): return lax.all_gather(part, 'dp', axis=0, tiled=True).astype(jnp.float32)  35 us
    convert_element_type x1, other arithmetic, local(): grad_scores = (exact * (grad_shares - centre)).astype(bf16)  30.1 us
    dot_general x1, matrix products, local(): jnp.einsum('qhd,khd->hqk', grad_mixed, values, preferred_element_type=f32)  27.2 us
    all_gather x2, blocking collectives, scatter_grad(): return lax.all_gather(part, 'dp', axis=0, tiled=True).astype(jnp.float32)  20.4 us
    sub x1, matrix products, local(): raised = jnp.exp(scores - largest)  19.8 us
  transfers between devices with their start and end apart: 10, of which 8 were waited for; matrix products, arithmetic and copies ran while one was open for 31% of the time, Pallas kernels for 0%

commit v1 on v0

--- a/solution.py
+++ b/solution.py
@@ -179,7 +179,8 @@
             grad_up_bias,
         ]
     )
-    small = lax.psum(small, ("dp", "tp"))
+    for axis in ("tp", "dp"):
+        small = lax.psum(small, axis)
     (
         sum_token,
         sum_gain1,

time: 804 us -> 804 us (level)
    psum x1 -> x2, blocking collectives: 40.5 us -> 41.2 us  [local(): small = lax.psum(small, axis)]
where the time goes in v1:
time: 804 us; the launch traced here: 800 us
  waiting for transfers between devices  386 us (48%)
  matrix products  186 us (23%)
  blocking collectives  88.3 us (11%)
  local copies, waits for them, and re-layouts  68.1 us (8%)
  other arithmetic  55.7 us (7%)
  between operations  15.4 us (2%)
    reduce_scatter x4, waiting for transfers between devices, scatter_grad(): lax.psum_scatter(partial, ('tp', 'dp'), scatter_dimension=0, tiled=True)  216 us
    all_gather x4, waiting for transfers between devices, gather_weight(): return lax.all_gather(own, ('tp', 'dp'), axis=0, tiled=True)  134 us
    psum x2, blocking collectives, local(): small = lax.psum(small, axis)  41.2 us
    all_gather x2, waiting for transfers between devices, scatter_grad(): return lax.all_gather(part, 'dp', axis=0, tiled=True).astype(jnp.float32)  35 us
    convert_element_type x1, other arithmetic, local(): grad_scores = (exact * (grad_shares - centre)).astype(bf16)  30.1 us
    dot_general x1, matrix products, local(): jnp.einsum('qhd,khd->hqk', grad_mixed, values, preferred_element_type=f32)  27.2 us
    all_gather x2, blocking collectives, scatter_grad(): return lax.all_gather(part, 'dp', axis=0, tiled=True).astype(jnp.float32)  20.3 us
    sub x1, matrix products, local(): raised = jnp.exp(scores - largest)  19.8 us
  transfers between devices with their start and end apart: 10, of which 8 were waited for; matrix products, arithmetic and copies ran while one was open for 31% of the time, Pallas kernels for 0%

profile of v1, /device:TPU:0, one launch (start us, length us, event | category | flops | bytes accessed | tf_op | source)
XLA Modules:
  0.0 799.6 jit_solution(3231710393818255993)
XLA Ops:
  7.4 1.2 constant_dynamic-slice_fusion.3
  8.6 0.8 copy.81
  9.5 1.4 constant_dynamic-slice_fusion.2
  10.9 0.7 constant_dynamic-slice_fusion.1
  11.7 1.6 constant_dynamic-slice_fusion
  13.4 0.7 compare_reduce_fusion
  14.1 0.7 dynamic-slice_reduce_fusion
  16.8 13.5 %all-gather = f32[4,3,128]{2,1,0:T(4,128)S(1)} all-gather(f32[1,3,128]{2,1,0:T(4,128)S(1)} %bitcast_convert_fusion), channel_id=1, replica_groups=mesh['dp'=8,'tp'=4] {'tp'}, dimensions={0}, use_global_device_ids=true | all-gather | bytes 7680 | tf_op jit(solution)/shard_map/all_gather | solution.py:95
  30.3 0.8 fusion.21
  31.2 0.9 multiply_reduce_fusion.9
  32.4 13.2 %all-gather.1 = f32[4,1,768]{2,1,0:T(1,128)S(1)} all-gather(f32[1,1,768]{2,1,0:T(1,128)S(1)} %reshape.247), channel_id=1, replica_groups=mesh['dp'=8,'tp'=4] {'tp'}, dimensions={0}, use_global_device_ids=true | all-gather | bytes 15360 | tf_op jit(solution)/shard_map/all_gather | solution.py:96
  45.6 30.0 %all-gather.9.cloned.1.call-done = bf16[3072,576]{1,0:T(8,128)(2,1)} async-done(((bf16[96,576]{1,0:T(8,128)(2,1)}), bf16[3072,576]{1,0:T(8,128)(2,1)}) %all-gather.9.cloned.1.call-update) | async-done | bytes 3538960 | tf_op jit(solution)/shard_map/all_gather | solution.py:47
  75.6 8.0 %copy.100 = bf16[4,768,576]{1,0,2:T(4,128)(2,1)} copy(bf16[4,768,576]{2,1,0:T(8,128)(2,1)} %bitcast.70) | data formatting | bytes 7077888 | tf_op jit(solution)/shard_map/reshape | solution.py:103
  83.6 2.5 copy.83
  86.1 1.7 copy-done.11
  87.8 5.3 add_convert_fusion
  93.1 6.4 copy.84
  99.5 19.8 %fusion.53 = (f32[12,832]{1,0:T(8,128)S(1)}, f32[12,832,832]{1,2,0:T(8,128)}) fusion(pred[832,832]{0,1:T(8,128)(4,1)S(1)} %broadcast_compare_fusion, bf16[832,12,192]{0,2,1:T(8,128)(2,1)} %bitcast.56), kind=kOutput, calls=%fused_computation.116 | convolution fusion | flops 1096483584 | bytes 36711424 | tf_op jit(solution)/shard_map/sub | solution.py:114
  119.3 16.0 %fusion.26 = bf16[12,64,832]{2,1,0:T(8,128)(2,1)} fusion(bf16[832,12,192]{0,2,1:T(8,128)(2,1)} %bitcast.57, f32[12,832,832]{1,2,0:T(8,128)} %get-tuple-element.74, f32[12,832]{1,0:T(8,128)S(1)} %get-tuple-element.73), kind=kOutput, calls=%fused_computation.62 | convolution fusion | flops 1080508416 | bytes 38476800 | tf_op jit(solution)/shard_map/hqk,khd->qhd/dot_general | solution.py:117
  135.3 4.9 fusion.50
  140.2 1.4 copy-done.4
  142.1 55.8 %all-gather.13.cloned.1.call-done = bf16[3072,768]{1,0:T(8,128)(2,1)} async-done(((bf16[96,768]{1,0:T(8,128)(2,1)}), bf16[3072,768]{1,0:T(8,128)(2,1)}) %all-gather.13.cloned.1.call-update) | async-done | bytes 4718608 | tf_op jit(solution)/shard_map/all_gather | solution.py:47
  197.9 6.6 copy.86
  204.5 10.7 %multiply_convert_fusion.1 = (bf16[832,3072]{1,0:T(8,128)(2,1)}, f32[832,3072]{1,0:T(8,128)}) fusion(f32[3072]{0:T(1024)S(1)} %bitcast.77, bf16[768,3072]{0,1:T(8,128)(2,1)} %bitcast.64, f32[832,768]{1,0:T(8,128)} %copy-done.4, f32[768]{0:T(1024)S(1)} %convert_element_type.165, f32[768]{0:T(1024)S(1)} %convert_element_type.164, f32[832]{0:T(1024)S(1)} %add_rsqrt_fusion, ...), kind=kOutput, calls=%fused_computation.18 | convolution fusion | flops 3944398848 | bytes 22635008 | tf_op jit(solution)/shard_map/dot_general | solution.py:124
  215.2 48.5 %all-gather.15.cloned.1.call-done = bf16[3072,768]{1,0:T(8,128)(2,1)} async-done(((bf16[96,768]{1,0:T(8,128)(2,1)}), bf16[3072,768]{1,0:T(8,128)(2,1)}) %all-gather.15.cloned.1.call-update) | async-done | bytes 4718608 | tf_op jit(solution)/shard_map/all_gather | solution.py:47
  263.7 11.2 %convert_reduce_fusion = (f32[3072]{0:T(1024)}, bf16[832,3072]{1,0:T(8,128)(2,1)S(1)}) fusion(f32[832,3072]{1,0:T(8,128)} %get-tuple-element.80, f32[3072]{0:T(1024)S(1)} %bitcast.78, bf16[3072,768]{1,0:T(8,128)(2,1)} %all-gather.15.cloned.1.call-done, bf16[832,768]{1,0:T(8,128)(2,1)S(1)} %copy-done.13, f32[768]{0:T(1024)S(1)} %convert_element_type.163, ...), kind=kOutput, calls=%fused_computation.17 | convolution fusion | flops 3961648128 | bytes 21362944 | tf_op jit(solution)/shard_map/dot_general | solution.py:135
  274.9 6.6 multiply_reduce_fusion.2
  281.5 7.7 convolution_convert_fusion.1
  289.2 7.1 convolution_convert_fusion
  296.2 9.7 %reshape.241 = bf16[768,4,768]{2,1,0:T(4,128)(2,1)} reshape(bf16[768,3072]{1,0:T(8,128)(2,1)} %convolution_convert_fusion.1) | data formatting | bytes 9437184 | tf_op jit(solution)/shard_map/reshape | solution.py:136
  306.0 5.1 copy.95
  311.2 4.9 multiply_reduce_fusion.3
  316.1 1.4 copy-done.6
  317.5 2.3 convolution_convert_fusion.3
  319.8 1.8 copy.87
  321.6 27.2 %multiply_reduce_fusion = (f32[12,832]{1,0:T(8,128)S(1)}, f32[12,832,832]{1,2,0:T(8,128)}) fusion(f32[12,832,832]{1,2,0:T(8,128)} %get-tuple-element.74, f32[12,832]{1,0:T(8,128)S(1)} %get-tuple-element.73, bf16[832,12,64]{0,2,1:T(8,128)(2,1)S(1)} %bitcast.74, bf16[832,12,192]{0,2,1:T(8,128)(2,1)} %bitcast.58), kind=kOutput, calls=%fused_computation.2 | convolution fusion | flops 1088166144 | bytes 71743488 | tf_op jit(solution)/shard_map/qhd,khd->hqk/dot_general | solution.py:150
  348.9 30.1 %multiply_convert_fusion = bf16[12,832,832]{1,2,0:T(8,128)(2,1)} fusion(f32[12,832,832]{1,2,0:T(8,128)} %get-tuple-element.78, f32[12,832]{1,0:T(8,128)S(1)} %get-tuple-element.77, f32[12,832,832]{1,2,0:T(8,128)} %get-tuple-element.74, f32[12,832]{1,0:T(8,128)S(1)} %get-tuple-element.73), kind=kLoop, calls=%fused_computation.1 | loop fusion | flops 33226752 | bytes 83146752 | tf_op jit(solution)/shard_map/convert_element_type | solution.py:152
  378.9 3.8 convolution_convert_fusion.4
  382.7 10.4 %multiply_bitcast_fusion = bf16[832,12,64]{0,2,1:T(8,128)(2,1)} fusion(bf16[12,832,832]{1,2,0:T(8,128)(2,1)} %multiply_convert_fusion, bf16[832,12,192]{0,2,1:T(8,128)(2,1)} %bitcast.59), kind=kOutput, calls=%fused_computation.31 | convolution fusion | flops 1064534016 | bytes 20545536 | tf_op jit(solution)/shard_map/hqk,qhd->khd/dot_general | solution.py:154
  393.1 15.3 %fusion.23 = bf16[832,12,64]{0,2,1:T(8,128)(2,1)} fusion(bf16[832,12,64]{0,2,1:T(8,128)(2,1)S(1)} %bitcast.75, f32[12,832,832]{1,2,0:T(8,128)} %get-tuple-element.74, f32[12,832]{1,0:T(8,128)S(1)} %get-tuple-element.73), kind=kOutput, calls=%fused_computation.61 | convolution fusion | flops 1079869440 | bytes 35822592 | tf_op jit(solution)/shard_map/hqk,qhd->khd/dot_general | solution.py:155
  408.5 10.0 %multiply_bitcast_fusion.1 = bf16[832,12,64]{0,2,1:T(8,128)(2,1)S(1)} fusion(bf16[12,832,832]{1,2,0:T(8,128)(2,1)} %multiply_convert_fusion, bf16[832,12,192]{0,2,1:T(8,128)(2,1)} %bitcast.60), kind=kOutput, calls=%fused_computation.32 | convolution fusion | flops 1064534016 | bytes 20545536 | tf_op jit(solution)/shard_map/hqk,khd->qhd/dot_general | solution.py:153
  418.6 1.1 convert_reduce_fusion.1
  419.7 1.9 copy-done.10
  421.7 6.5 convolution_convert_fusion.2
  428.2 5.8 copy.91
  434.0 6.0 copy.103
  440.7 9.7 %fusion.62 = f32[832,768]{1,0:T(8,128)} fusion(bf16[832,3072]{1,0:T(8,128)(2,1)} %get-tuple-element.79, bf16[3072,768]{1,0:T(8,128)(2,1)} %all-gather.15.cloned.1.call-done), kind=kOutput, calls=%fused_computation.117 | convolution fusion | flops 3925868544 | bytes 12386304 | tf_op jit(solution)/shard_map/dot_general | solution.py:127
  450.8 11.4 %multiply_reduce_fusion.4 = (f32[768]{0:T(1024)S(1)}, f32[832]{0:T(1024)S(1)}, f32[832]{0:T(1024)S(1)}, f32[768]{0:T(1024)S(1)}, f32[768]{0:T(1024)S(1)}, /*inde...) fusion(bf16[832,768]{1,0:T(8,128)(2,1)S(1)} %copy-done.3, f32[832]{0:T(1024)S(1)} %copy-done.30, ...), kind=kOutput, calls=%fused_computation.36 | convolution fusion | flops 2960371200 | bytes 18922240 | tf_op jit(solution)/shard_map/dot_general | solution.py:161
  462.3 2.9 multiply_reduce_fusion.5
  465.2 64.2 %reduce-scatter.11.cloned.1.call-done = bf16[96,768]{1,0:T(8,128)(2,1)} async-done(((bf16[3072,768]{1,0:T(8,128)(2,1)}), bf16[96,768]{1,0:T(8,128)(2,1)}) %reduce-scatter.11.cloned.1.call-update) | async-done | bytes 147472 | tf_op jit(solution)/shard_map/reduce_scatter | solution.py:52
  529.7 18.5 %psum.14 = f32[12288]{0:T(1024)S(1)} all-reduce(f32[12288]{0:T(1024)S(1)} %constant_dynamic-update-slice_fusion), channel_id=1, replica_groups=mesh['dp'=8,'tp'=4] {'tp'}, use_global_device_ids=true, to_apply=%region_22.23 | all-reduce | flops 12288 | bytes 98304 | tf_op jit(solution)/shard_map/psum | solution.py:183
  548.2 22.7 %psum.15 = f32[12288]{0:T(1024)S(1)} all-reduce(f32[12288]{0:T(1024)S(1)} %psum.14), channel_id=1, replica_groups=mesh['dp'=8,'tp'=4] {'dp'}, use_global_device_ids=true, to_apply=%region_23.24 | all-reduce | flops 12288 | bytes 98304 | tf_op jit(solution)/shard_map/psum | solution.py:183
  571.0 0.7 dynamic_slice.27
  573.0 3.4 broadcast_multiply_fusion
  576.4 54.0 %reduce-scatter.7.cloned.1.call-done = bf16[24,768]{1,0:T(8,128)(2,1)} async-done(((bf16[768,768]{1,0:T(8,128)(2,1)}), bf16[24,768]{1,0:T(8,128)(2,1)}) %reduce-scatter.7.cloned.1.call-update) | async-done | bytes 36880 | tf_op jit(solution)/shard_map/reduce_scatter | solution.py:52
  630.4 9.5 %all_gather.37 = bf16[192,768]{1,0:T(8,128)(2,1)S(1)} all-gather(bf16[24,768]{1,0:T(8,128)(2,1)} %reduce-scatter.7.cloned.1.call-done), channel_id=1, replica_groups=mesh['dp'=8,'tp'=4] {'dp'}, dimensions={0}, use_global_device_ids=true | all-gather | bytes 331776 | tf_op jit(solution)/shard_map/all_gather | solution.py:53
  640.0 0.9 convert_element_type.183
  640.8 98.1 %reduce-scatter.13.cloned.1.call-done = bf16[96,576]{1,0:T(8,128)(2,1)} async-done(((bf16[3072,576]{1,0:T(8,128)(2,1)}), bf16[96,576]{1,0:T(8,128)(2,1)}) %reduce-scatter.13.cloned.1.call-update) | async-done | bytes 110608 | tf_op jit(solution)/shard_map/reduce_scatter | solution.py:52
  738.9 10.8 %all_gather.36 = bf16[768,576]{1,0:T(8,128)(2,1)S(1)} all-gather(bf16[96,576]{1,0:T(8,128)(2,1)} %reduce-scatter.13.cloned.1.call-done), channel_id=1, replica_groups=mesh['dp'=8,'tp'=4] {'dp'}, dimensions={0}, use_global_device_ids=true | all-gather | bytes 995328 | tf_op jit(solution)/shard_map/all_gather | solution.py:53
  750.4 1.4 convert.2
  751.7 12.1 %all-gather.17.cloned.1.call-done = bf16[768,768]{1,0:T(8,128)(2,1)} async-done(((bf16[96,768]{1,0:T(8,128)(2,1)}), bf16[768,768]{1,0:T(8,128)(2,1)}) %all-gather.17.cloned.1.call-update) | async-done | bytes 1179664 | tf_op jit(solution)/shard_map/all_gather | solution.py:53
  763.9 2.9 convert_element_type.185
  766.8 22.9 %all-gather.19.cloned.1.call-done = bf16[768,768]{1,0:T(8,128)(2,1)} async-done(((bf16[96,768]{1,0:T(8,128)(2,1)}), bf16[768,768]{1,0:T(8,128)(2,1)}) %all-gather.19.cloned.1.call-update) | async-done | bytes 1179664 | tf_op jit(solution)/shard_map/all_gather | solution.py:53
  789.7 2.8 convert_element_type.187
  (177 shorter events, 6.3 us)
Async XLA Ops:
  7.2 3.7 copy-start
  7.2 9.3 %copy-start.49 = (bf16[3,128]{1,0:T(4,128)(2,1)S(1)}, bf16[3,128]{1,0:T(4,128)(2,1)}, u32[]{:S(2)}) copy-start(bf16[3,128]{1,0:T(4,128)(2,1)} %param.26) | copy-start | bytes 2308
  7.2 9.3 %copy-start.48 = (bf16[768]{0:T(1024)(128)(2,1)S(1)}, bf16[768]{0:T(1024)(128)(2,1)}, u32[]{:S(2)}) copy-start(bf16[768]{0:T(1024)(128)(2,1)} %param.33) | copy-start | bytes 4612
  7.2 9.3 %copy-start.39 = (bf16[768]{0:T(1024)(128)(2,1)S(1)}, bf16[768]{0:T(1024)(128)(2,1)}, u32[]{:S(2)}) copy-start(bf16[768]{0:T(1024)(128)(2,1)} %param.22) | copy-start | bytes 4612
  7.2 9.4 %copy-start.40 = (bf16[768]{0:T(1024)(128)(2,1)S(1)}, bf16[768]{0:T(1024)(128)(2,1)}, u32[]{:S(2)}) copy-start(bf16[768]{0:T(1024)(128)(2,1)} %param.23) | copy-start | bytes 4612
  7.3 9.4 %copy-start.41 = (bf16[768]{0:T(1024)(128)(2,1)S(1)}, bf16[768]{0:T(1024)(128)(2,1)}, u32[]{:S(2)}) copy-start(bf16[768]{0:T(1024)(128)(2,1)} %param.29) | copy-start | bytes 4612
  7.3 9.4 %copy-start.42 = (bf16[768]{0:T(1024)(128)(2,1)S(1)}, bf16[768]{0:T(1024)(128)(2,1)}, u32[]{:S(2)}) copy-start(bf16[768]{0:T(1024)(128)(2,1)} %param.30) | copy-start | bytes 4612
  7.3 9.4 %copy-start.43 = (bf16[768]{0:T(1024)(128)(2,1)S(1)}, bf16[768]{0:T(1024)(128)(2,1)}, u32[]{:S(2)}) copy-start(bf16[768]{0:T(1024)(128)(2,1)} %param.36) | copy-start | bytes 4612
  7.3 9.4 %copy-start.44 = (bf16[768]{0:T(1024)(128)(2,1)S(1)}, bf16[768]{0:T(1024)(128)(2,1)}, u32[]{:S(2)}) copy-start(bf16[768]{0:T(1024)(128)(2,1)} %param.24) | copy-start | bytes 4612
  7.3 9.4 %copy-start.45 = (bf16[768]{0:T(1024)(128)(2,1)S(1)}, bf16[768]{0:T(1024)(128)(2,1)}, u32[]{:S(2)}) copy-start(bf16[768]{0:T(1024)(128)(2,1)} %param.28) | copy-start | bytes 4612
  7.3 9.5 %copy-start.46 = (bf16[768]{0:T(1024)(128)(2,1)S(1)}, bf16[768]{0:T(1024)(128)(2,1)}, u32[]{:S(2)}) copy-start(bf16[768]{0:T(1024)(128)(2,1)} %param.31) | copy-start | bytes 4612
  7.3 23.0 %copy-start.2 = (bf16[832,768]{1,0:T(8,128)(2,1)S(1)}, bf16[832,768]{1,0:T(8,128)(2,1)}, u32[]{:S(2)}) copy-start(bf16[832,768]{1,0:T(8,128)(2,1)} %param.19) | copy-start | bytes 3833860
  7.3 68.2 %all-gather.9.cloned.1.call-start = ((), (), s32[]{:S(2)}) async-start(), calls=%async_computation.4 | async-start | bytes 4055040 | tf_op jit(solution)/shard_map/all_gather | solution.py:47
  9.4 125.9 %all-gather.11.cloned.1.call-start = ((), (), s32[]{:S(2)}) async-start(), calls=%async_computation.5 | async-start | bytes 1216512 | tf_op jit(solution)/shard_map/all_gather | solution.py:47
  10.9 187.0 %all-gather.13.cloned.1.call-start = ((), (), s32[]{:S(2)}) async-start(), calls=%async_computation.6 | async-start | bytes 4866048 | tf_op jit(solution)/shard_map/all_gather | solution.py:47
  11.7 252.0 %all-gather.15.cloned.1.call-start = ((), (), s32[]{:S(2)}) async-start(), calls=%async_computation.7 | async-start | bytes 4866048 | tf_op jit(solution)/shard_map/all_gather | solution.py:47
  13.3 437.1 %reduce-scatter.9.cloned.1.call-start = ((), (), s32[]{:S(2)}) async-start(), calls=%async_computation.9 | async-start | bytes 4866048 | tf_op jit(solution)/shard_map/reduce_scatter | solution.py:52
  14.1 121.2 %copy-start.16 = (f32[832]{0:T(1024)}, f32[832]{0:T(1024)S(1)}, u32[]{:S(2)}) copy-start(f32[832]{0:T(1024)S(1)} %convert_element_type.150) | copy-start | bytes 9988
  15.4 295.8 %copy-start.14 = (f32[832]{0:T(1024)}, f32[832]{0:T(1024)S(1)}, u32[]{:S(2)}) copy-start(f32[832]{0:T(1024)S(1)} %convert_element_type.149) | copy-start | bytes 9988
  16.0 119.3 %copy-start.18 = (f32[832]{0:T(1024)}, f32[832]{0:T(1024)S(1)}, u32[]{:S(2)}) copy-start(f32[832]{0:T(1024)S(1)} %get-tuple-element.72) | copy-start | bytes 9988
  16.6 118.7 %copy-start.20 = (f32[768]{0:T(1024)}, f32[768]{0:T(1024)S(1)}, u32[]{:S(2)}) copy-start(f32[768]{0:T(1024)S(1)} %convert_element_type.151) | copy-start | bytes 9220
  16.6 69.4 %copy-start.27 = (f32[768]{0:T(1024)}, f32[768]{0:T(1024)S(1)}, u32[]{:S(2)}) copy-start(f32[768]{0:T(1024)S(1)} %convert_element_type.154) | copy-start | bytes 9220
  16.7 272.4 %copy-start.33 = (f32[768]{0:T(1024)}, f32[768]{0:T(1024)S(1)}, u32[]{:S(2)}) copy-start(f32[768]{0:T(1024)S(1)} %convert_element_type.163) | copy-start | bytes 9220
  16.7 69.3 %copy-start.35 = (f32[768]{0:T(1024)}, f32[768]{0:T(1024)S(1)}, u32[]{:S(2)}) copy-start(f32[768]{0:T(1024)S(1)} %convert_element_type.155) | copy-start | bytes 9220
  31.2 54.9 %copy-start.22 = (f32[832]{0:T(1024)}, f32[832]{0:T(1024)S(1)}, u32[]{:S(2)}) copy-start(f32[832]{0:T(1024)S(1)} %broadcast_multiply_fusion.6) | copy-start | bytes 9988
  32.1 54.0 %copy-start.29 = (f32[832]{0:T(1024)}, f32[832]{0:T(1024)S(1)}, u32[]{:S(2)}) copy-start(f32[832]{0:T(1024)S(1)} %add_rsqrt_fusion.1) | copy-start | bytes 9988
  86.1 1.7 copy-start.11
  140.2 1.4 copy-start.4
  204.5 59.2 %copy-start.13 = (bf16[832,768]{1,0:T(8,128)(2,1)S(1)}, bf16[832,768]{1,0:T(8,128)(2,1)}, u32[]{:S(2)}) copy-start(bf16[832,768]{1,0:T(8,128)(2,1)} %param.37) | copy-start | bytes 3833860
  204.5 70.4 %slice-start = ((s8[4718592]{0:T(1024)(128)(4,1)}), s8[524288]{0:T(1024)(128)(4,1)S(1)}, s32[]{:S(2)}) async-start(s8[4718592]{0:T(1024)(128)(4,1)} %bitcast.65), calls=%async_computation.14 | async-start | bytes 1048576
  263.7 11.2 %copy-start.5 = (f32[832,768]{1,0:T(8,128)S(1)}, f32[832,768]{1,0:T(8,128)}, u32[]{:S(2)}) copy-start(f32[832,768]{1,0:T(8,128)} %copy-done.4) | copy-start | bytes 7667716
  263.7 11.2 %slice-start.1 = ((s8[4718592]{0:T(1024)(128)(4,1)}), s8[4194304]{0:T(1024)(128)(4,1)S(1)}, s32[]{:S(2)}) async-start(s8[4718592]{0:T(1024)(128)(4,1)} %bitcast.65), calls=%async_computation.15 | async-start | bytes 8388608
  281.5 7.7 copy-start.51
  311.1 218.3 %reduce-scatter.11.cloned.1.call-start = ((), (), s32[]{:S(2)}) async-start(), calls=%async_computation.11 | async-start | bytes 4866048 | tf_op jit(solution)/shard_map/reduce_scatter | solution.py:52
  311.2 6.4 copy-start.50
  316.1 1.4 copy-start.6
  348.8 281.6 %reduce-scatter.7.cloned.1.call-start = ((), (), s32[]{:S(2)}) async-start(), calls=%async_computation.8 | async-start | bytes 1216512 | tf_op jit(solution)/shard_map/reduce_scatter | solution.py:52
  348.8 30.1 %copy-start.7 = (f32[832,768]{1,0:T(8,128)S(1)}, f32[832,768]{1,0:T(8,128)}, u32[]{:S(2)}) copy-start(f32[832,768]{1,0:T(8,128)} %copy-done.6) | copy-start | bytes 7667716
  408.5 330.5 %reduce-scatter.13.cloned.1.call-start = ((), (), s32[]{:S(2)}) async-start(), calls=%async_computation.13 | async-start | bytes 4055040 | tf_op jit(solution)/shard_map/reduce_scatter | solution.py:52
  408.5 10.0 %copy-start.9 = (bf16[832,12,64]{0,2,1:T(8,128)(2,1)S(1)}, bf16[832,12,64]{0,2,1:T(8,128)(2,1)}, u32[]{:S(2)}) copy-start(bf16[832,12,64]{0,2,1:T(8,128)(2,1)} %multiply_bitcast_fusion) | copy-start | bytes 3833860
  408.5 10.0 %copy-start.12 = (bf16[832,12,64]{0,2,1:T(8,128)(2,1)S(1)}, bf16[832,12,64]{0,2,1:T(8,128)(2,1)}, u32[]{:S(2)}) copy-start(bf16[832,12,64]{0,2,1:T(8,128)(2,1)} %fusion.23) | copy-start | bytes 3833860
  418.5 3.1 copy-start.3
  418.5 3.1 copy-start.15
  418.5 3.1 copy-start.17
  418.5 3.1 copy-start.19
  418.6 3.1 copy-start.21
  418.6 3.1 copy-start.23
  418.6 3.0 copy-start.28
  418.6 3.0 copy-start.30
  418.6 3.0 copy-start.36
  419.7 1.9 copy-start.10
  440.0 0.7 copy-start.47
  440.1 323.8 %all-gather.17.cloned.1.call-start = ((), (), s32[]{:S(2)}) async-start(), calls=%async_computation.10 | async-start | bytes 1327104 | tf_op jit(solution)/shard_map/all_gather | solution.py:53
  440.7 10.0 %copy-start.34 = (f32[768]{0:T(1024)S(1)}, f32[768]{0:T(1024)}, u32[]{:S(2)}) copy-start(f32[768]{0:T(1024)} %copy-done.33) | copy-start | bytes 9220
  450.4 11.8 %copy-start.26 = (f32[832]{0:T(1024)S(1)}, f32[832]{0:T(1024)}, u32[]{:S(2)}) copy-start(f32[832]{0:T(1024)} %get-tuple-element.53) | copy-start | bytes 9988
  450.5 339.2 %all-gather.19.cloned.1.call-start = ((), (), s32[]{:S(2)}) async-start(), calls=%async_computation.12 | async-start | bytes 1327104 | tf_op jit(solution)/shard_map/all_gather | solution.py:53
  450.8 11.5 %copy-start.8 = (f32[832,768]{1,0:T(8,128)S(1)}, f32[832,768]{1,0:T(8,128)}, u32[]{:S(2)}) copy-start(f32[832,768]{1,0:T(8,128)} %copy-done.6) | copy-start | bytes 7667716
  462.2 67.3 %copy-start.25 = (f32[768]{0:T(1024)S(1)}, f32[768]{0:T(1024)}, u32[]{:S(2)}) copy-start(f32[768]{0:T(1024)} %get-tuple-element.42) | copy-start | bytes 9220
  462.3 67.3 %copy-start.24 = (f32[768]{0:T(1024)S(1)}, f32[768]{0:T(1024)}, u32[]{:S(2)}) copy-start(f32[768]{0:T(1024)} %get-tuple-element.41) | copy-start | bytes 9220
  462.3 67.3 %copy-start.38 = (f32[768]{0:T(1024)S(1)}, f32[768]{0:T(1024)}, u32[]{:S(2)}) copy-start(f32[768]{0:T(1024)} %get-tuple-element.34) | copy-start | bytes 9220
  462.3 67.3 %copy-start.37 = (f32[768]{0:T(1024)S(1)}, f32[768]{0:T(1024)}, u32[]{:S(2)}) copy-start(f32[768]{0:T(1024)} %get-tuple-element.40) | copy-start | bytes 9220
  462.3 67.4 %copy-start.32 = (f32[3072]{0:T(1024)S(1)}, f32[3072]{0:T(1024)}, u32[]{:S(2)}) copy-start(f32[3072]{0:T(1024)} %get-tuple-element.82) | copy-start | bytes 36868
  462.3 110.7 %copy-start.31 = (f32[832]{0:T(1024)S(1)}, f32[832]{0:T(1024)}, u32[]{:S(2)}) copy-start(f32[832]{0:T(1024)} %get-tuple-element.71) | copy-start | bytes 9988
  763.9 28.7 %copy-start.1 = (bf16[768,768]{1,0:T(8,128)(2,1)S(1)}, bf16[768,768]{1,0:T(8,128)(2,1)}, u32[]{:S(2)}) copy-start(bf16[768,768]{1,0:T(8,128)(2,1)} %param.32) | copy-start | bytes 3538948
Sparse Core Ops, SparseCore 0:
  11.6 63.8 all-gather.8
  79.0 52.7 all-gather.10
  135.2 62.5 all-gather.12
  201.2 62.4 all-gather.14
  311.2 105.7 reduce-scatter.8
  423.3 106.0 reduce-scatter.10
  535.1 95.3 reduce-scatter.6
  635.8 103.0 reduce-scatter.12
  740.8 22.9 all-gather.16
  765.6 24.0 all-gather.18
